TPU v7x, 32 devices: a whole 2x2x4 slice. The times are simulated.
32 devices in a mesh: groups: 2 (over x), space: 16 (over z, y, core).
Axes of the slice: x: 2, y: 2, z: 4, core: 2. Of those that a mesh axis runs over, the one named last changes fastest.
Arguments:
- volume: bfloat16 [64, 64, 32, 64], P(('groups', 'space')), parts along dimension 0, may hold values from -6 to 6
- weight_one: bfloat16 [3, 3, 3, 64, 64], replicated, may hold values from -0.15625 to 0.15625
- weight_two: bfloat16 [3, 3, 3, 64, 128], replicated, may hold values from -0.15625 to 0.15625
- cotangent: bfloat16 [64, 64, 32, 128], P(('groups', 'space')), parts along dimension 0, may hold values from -6 to 6
Outputs:
- output: float32 [64, 64, 32, 128], P(('groups', 'space')), parts along dimension 0
- grad_volume: float32 [64, 64, 32, 64], P(('groups', 'space')), parts along dimension 0
- grad_one: float32 [6, 3, 3, 64, 64], P('groups', None, None, None, 'space'), parts along dimension 0
- grad_two: float32 [6, 3, 3, 64, 128], P('groups', None, None, None, 'space'), parts along dimension 0
There are 2 independent parts, one for each index of `groups`. A program takes and returns all parts, laid end to end along the dimension named above; an argument that names none is the same for every part. Nothing has to cross between parts.
All inputs are finite; a program needn't handle non-finite values.
Results may differ from a plain program's by a relative error of at most 0.0029.
Values may be sent and summed in bfloat16 or wider, within the bound.
A program may use at most 64 MiB of HBM per device.

v0:
```python
import functools
import math

import jax
import jax.numpy as jnp
from jax import lax
from jax.experimental import pallas as pl
from jax.experimental.pallas import tpu as pltpu
from jax.sharding import PartitionSpec as P

MESH = pl.DeviceIdType.MESH
F32 = jnp.float32
BF16 = jnp.bfloat16
TN = (((0,), (0,)), ((), ()))


def kernel(
    n, planes, height, width, ci, cm, co, scale,
    vol, cot, w1, w2, w1f, wg,
    out, gvol, g1, g2,
    pv, pa, pg, ct, vraw, araw, graw, vh, ah, gh, dsl, acc1, acc2, tx, rx,
    loc_sem, hs_sem, hr_sem, ts_sem, tr_sem,
):
    me = lax.axis_index("space")
    plane = height * width
    chunk = plane // 4
    pad = plane + 2 * width
    r1, r2 = cm // n, co // n

    barrier = pltpu.get_barrier_semaphore()
    for j in range(1, n):
        pl.semaphore_signal(
            barrier, inc=1, device_id={"space": lax.rem(me + j, n)}, device_id_type=MESH
        )

    local = [pltpu.make_async_copy(vol, vraw, loc_sem.at[0])]
    for p in range(planes):
        local.append(
            pltpu.make_async_copy(
                cot.at[pl.ds(p * plane, plane)],
                ct.at[p + 1, pl.ds(width, plane)],
                loc_sem.at[1 + p],
            )
        )
    for copy in local:
        copy.start()

    for ref in (pv, pa, pg, ct):
        zero = jnp.zeros((width, ref.shape[2]), BF16)
        for p in range(planes + 2):
            ref[p, pl.ds(0, width), :] = zero
            ref[p, pl.ds(pad - width, width), :] = zero

    column = lax.broadcasted_iota(jnp.int32, (chunk, 1), 0) % width
    first = column == 0
    last = column == width - 1

    def spread(x, ref, p, row):
        back = jnp.where(first, 0.0, pltpu.roll(x, 1, 0))
        ahead = jnp.where(last, 0.0, pltpu.roll(x, chunk - 1, 0))
        ref[p, pl.ds(row, chunk), :] = jnp.concatenate([back, x, ahead], axis=1).astype(BF16)

    def each(count, body):
        def step(k, carry):
            body(k // 4, pl.multiple_of(lax.rem(k, 4) * chunk, chunk))
            return carry

        lax.fori_loop(0, 4 * count, step, 0)

    def halo(kind, low_src, high_src, low_dst, high_dst):
        left = pltpu.make_async_remote_copy(
            low_src, high_dst, hs_sem.at[kind, 0], hr_sem.at[kind, 0],
            device_id={"space": lax.rem(me + n - 1, n)}, device_id_type=MESH,
        )
        right = pltpu.make_async_remote_copy(
            high_src, low_dst, hs_sem.at[kind, 1], hr_sem.at[kind, 1],
            device_id={"space": lax.rem(me + 1, n)}, device_id_type=MESH,
        )

        def start():
            @pl.when(me > 0)
            def _():
                left.start()

            @pl.when(me < n - 1)
            def _():
                right.start()

        def wait_recv():
            @pl.when(me < n - 1)
            def _():
                left.wait_recv()

            @pl.when(me == n - 1)
            def _():
                high_dst[...] = jnp.zeros(high_dst.shape, BF16)

            @pl.when(me > 0)
            def _():
                right.wait_recv()

            @pl.when(me == 0)
            def _():
                low_dst[...] = jnp.zeros(low_dst.shape, BF16)

        def wait_send():
            @pl.when(me > 0)
            def _():
                left.wait_send()

            @pl.when(me < n - 1)
            def _():
                right.wait_send()

        return start, wait_recv, wait_send

    end = (planes - 1) * plane
    volume_halo = halo(
        0, vol.at[pl.ds(0, plane)], vol.at[pl.ds(end, plane)], vh.at[0], vh.at[1]
    )
    cot_halo = halo(
        1, cot.at[pl.ds(0, plane)], cot.at[pl.ds(end, plane)],
        ct.at[0, pl.ds(width, plane)], ct.at[planes + 1, pl.ds(width, plane)],
    )
    act_halo = halo(
        2, araw.at[pl.ds(0, plane)], araw.at[pl.ds(end, plane)], ah.at[0], ah.at[1]
    )
    grad_halo = halo(
        3, graw.at[pl.ds(0, plane)], graw.at[pl.ds(end, plane)], gh.at[0], gh.at[1]
    )

    pl.semaphore_wait(barrier, n - 1)
    volume_halo[0]()
    cot_halo[0]()

    local[0].wait()

    def own_volume(p, row):
        x = vraw[pl.ds(pl.multiple_of(p * plane + row, chunk), chunk), :].astype(F32)
        spread(x, pv, p + 1, row + width)

    each(planes, own_volume)

    def halo_planes(slots, ref):
        def body(p, row):
            x = slots[p, pl.ds(row, chunk), :].astype(F32)
            spread(x, ref, p * (planes + 1), row + width)

        each(2, body)

    def conv(ref, kernels, p, row):
        total = None
        for a in range(3):
            for b in range(3):
                term = jnp.dot(
                    ref[p + a, pl.ds(pl.multiple_of(row + b * width, width), chunk), :],
                    kernels[a * 3 + b],
                    preferred_element_type=F32,
                )
                total = term if total is None else total + term
        return total

    volume_halo[1]()
    halo_planes(vh, pv)

    def first_conv(p, row):
        hidden = conv(pv, w1, p, row)
        s = jax.nn.sigmoid(hidden)
        at = pl.ds(pl.multiple_of(p * plane + row, chunk), chunk)
        dsl[at, :] = s * (1.0 + hidden * (1.0 - s))
        rounded = (hidden * s).astype(BF16)
        araw[at, :] = rounded
        spread(rounded.astype(F32), pa, p + 1, row + width)

    each(planes, first_conv)
    act_halo[0]()

    for copy in local[1:]:
        copy.wait()
    cot_halo[1]()
    low_lanes = lax.broadcasted_iota(jnp.int32, (1, 2 * cm), 1) < cm

    def back_conv(p, row):
        pieces = [
            ct[p + a, pl.ds(pl.multiple_of(row + b * width, width), chunk), :]
            for a in range(3)
            for b in range(3)
        ]
        y = jnp.dot(jnp.concatenate(pieces, axis=1), wg[...], preferred_element_type=F32)
        z = y[:, : 2 * cm]
        z = jnp.where(
            low_lanes,
            jnp.where(first, 0.0, pltpu.roll(z, 1, 0)),
            jnp.where(last, 0.0, pltpu.roll(z, chunk - 1, 0)),
        )
        grad_act = z[:, :cm] + z[:, cm:] + y[:, 2 * cm :]
        at = pl.ds(pl.multiple_of(p * plane + row, chunk), chunk)
        rounded = (grad_act * dsl[at, :]).astype(BF16)
        graw[at, :] = rounded
        spread(rounded.astype(F32), pg, p + 1, row + width)

    each(planes, back_conv)
    grad_halo[0]()

    act_halo[1]()
    halo_planes(ah, pa)

    acc1[...] = jnp.zeros(acc1.shape, F32)
    acc2[...] = jnp.zeros(acc2.shape, F32)

    def kernel_terms(p, row):
        at = pl.ds(pl.multiple_of(p * plane + row, chunk), chunk)
        field2 = ct[p + 1, pl.ds(pl.multiple_of(row + width, width), chunk), :].T
        field1 = graw[at, :].T
        for a in range(3):
            for b in range(3):
                rows = pl.ds(pl.multiple_of(row + b * width, width), chunk)
                acc2[a * 3 + b] += jnp.dot(field2, pa[p + a, rows, :], preferred_element_type=F32)
                acc1[a * 3 + b] += jnp.dot(field1, pv[p + a, rows, :], preferred_element_type=F32)

    each(planes, kernel_terms)

    blank = jnp.zeros((tx.shape[2] - r1 - r2, 3 * ci), F32)
    for t in range(9):
        for s in range(n):
            tile = jnp.concatenate(
                [
                    acc2[t, pl.ds(s * r2, r2), :],
                    acc1[t, pl.ds(s * r1, r1), :],
                    blank,
                ],
                axis=0,
            ).astype(BF16)
            tx[s, t] = tile[:, : 2 * ci]
            tx[s, 9 + t // 2, :, pl.ds((t % 2) * ci, ci)] = tile[:, 2 * ci :]
    for s in range(n):
        tx[s, 13, :, pl.ds(ci, ci)] = jnp.zeros((tx.shape[2], ci), BF16)

    sends = []
    for j in range(1, n):
        owner = lax.rem(me + j, n)
        sends.append(
            pltpu.make_async_remote_copy(
                tx.at[owner], rx.at[j], ts_sem.at[j], tr_sem.at[j],
                device_id={"space": owner}, device_id_type=MESH,
            )
        )
        sends[-1].start()

    def second_conv(p, row):
        at = pl.ds(pl.multiple_of(p * plane + row, chunk), chunk)
        out[at, :] = conv(pa, w2, p, row)

    each(planes, second_conv)

    grad_halo[1]()
    halo_planes(gh, pg)

    def last_conv(p, row):
        at = pl.ds(pl.multiple_of(p * plane + row, chunk), chunk)
        gvol[at, :] = conv(pg, w1f, p, row)

    each(planes, last_conv)

    for send in sends:
        send.wait_recv()
    for t in range(14):
        total = tx[me, t].astype(F32)
        for j in range(1, n):
            total = total + rx[j, t].astype(F32)
        total = total * scale
        taps = (3 * t, 3 * t + 1) if t < 9 else (3 * (2 * (t - 9)) + 2, 3 * (2 * (t - 9) + 1) + 2)
        for half, tap in enumerate(taps):
            if tap < 27:
                part = total[:, half * ci : (half + 1) * ci]
                g2[tap] = part[:r2]
                g1[tap] = part[r2 : r2 + r1]

    for send in sends:
        send.wait_send()
    for exchange in (volume_halo, cot_halo, act_halo, grad_halo):
        exchange[2]()


def shards(volume, weight_one, weight_two, cotangent):
    n = lax.axis_size("space")
    planes, height, width, ci = volume.shape
    cm, co = weight_two.shape[3], weight_two.shape[4]
    plane = height * width
    cells = planes * plane
    pad = plane + 2 * width
    scale = 1.0 / math.sqrt(cells * n)

    w1 = weight_one.reshape(9, 3 * ci, cm)
    w2 = weight_two.reshape(9, 3 * cm, co)
    w1f = jnp.transpose(weight_one[::-1, ::-1, ::-1], (0, 1, 2, 4, 3)).reshape(9, 3 * cm, ci)
    wg = jnp.transpose(weight_two[::-1, ::-1, ::-1], (0, 1, 4, 2, 3))
    wg = jnp.concatenate([wg[:, :, :, 0], wg[:, :, :, 2], wg[:, :, :, 1]], axis=3)
    wg = wg.reshape(9 * co, 3 * cm)

    vmem = pl.BlockSpec(memory_space=pltpu.VMEM)
    hbm = pl.BlockSpec(memory_space=pl.ANY)
    rows = -(-(cm // n + co // n) // 16) * 16
    out, gvol, g1, g2 = pl.pallas_call(
        functools.partial(kernel, n, planes, height, width, ci, cm, co, scale),
        out_shape=(
            jax.ShapeDtypeStruct((cells, co), F32),
            jax.ShapeDtypeStruct((cells, ci), F32),
            jax.ShapeDtypeStruct((27, cm // n, ci), F32),
            jax.ShapeDtypeStruct((27, co // n, cm), F32),
        ),
        in_specs=[hbm, hbm, vmem, vmem, vmem, vmem],
        out_specs=(vmem, vmem, vmem, vmem),
        scratch_shapes=[
            pltpu.VMEM((planes + 2, pad, 3 * ci), BF16),
            pltpu.VMEM((planes + 2, pad, 3 * cm), BF16),
            pltpu.VMEM((planes + 2, pad, 3 * cm), BF16),
            pltpu.VMEM((planes + 2, pad, co), BF16),
            pltpu.VMEM((cells, ci), BF16),
            pltpu.VMEM((cells, cm), BF16),
            pltpu.VMEM((cells, cm), BF16),
            pltpu.VMEM((2, plane, ci), BF16),
            pltpu.VMEM((2, plane, cm), BF16),
            pltpu.VMEM((2, plane, cm), BF16),
            pltpu.VMEM((cells, cm), F32),
            pltpu.VMEM((9, cm, 3 * ci), F32),
            pltpu.VMEM((9, co, 3 * cm), F32),
            pltpu.VMEM((n, 14, rows, 2 * ci), BF16),
            pltpu.VMEM((n, 14, rows, 2 * ci), BF16),
            pltpu.SemaphoreType.DMA((1 + planes,)),
            pltpu.SemaphoreType.DMA((4, 2)),
            pltpu.SemaphoreType.DMA((4, 2)),
            pltpu.SemaphoreType.DMA((n,)),
            pltpu.SemaphoreType.DMA((n,)),
        ],
        compiler_params=pltpu.CompilerParams(
            collective_id=0, has_side_effects=True, vmem_limit_bytes=60 << 20
        ),
    )(
        volume.reshape(cells, ci), cotangent.reshape(cells, co), w1, w2, w1f, wg
    )
    return (
        out.reshape(planes, height, width, co),
        gvol.reshape(planes, height, width, ci),
        jnp.transpose(g1.reshape(3, 3, 3, cm // n, ci), (0, 1, 2, 4, 3)),
        jnp.transpose(g2.reshape(3, 3, 3, co // n, cm), (0, 1, 2, 4, 3)),
    )


def solution(mesh):
    return jax.shard_map(
        shards,
        mesh=mesh,
        in_specs=(
            P(("groups", "space"), None, None, None),
            P(),
            P(),
            P(("groups", "space"), None, None, None),
        ),
        out_specs=(
            P(("groups", "space"), None, None, None),
            P(("groups", "space"), None, None, None),
            P("groups", None, None, None, "space"),
            P("groups", None, None, None, "space"),
        ),
        check_vma=False,
    )
```

profile of v0, /device:TPU:1, one launch (start us, length us, event | category | flops | bytes accessed | tf_op | source)
XLA Modules:
  0.0 88.2 jit_solution(15723659444594394850)
XLA Ops:
  0.6 0.0 copy-start.1
  0.6 1.1 %reverse_bitcast_fusion.1 = bf16[3,3,3,64,64]{3,4,2,1,0:T(8,128)(2,1)S(1)} fusion(bf16[3,3,3,64,64]{4,3,2,1,0:T(8,128)(2,1)} %param.5), kind=kLoop, calls=%fused_computation.2 | loop fusion | bytes 442368 | tf_op jit(solution)/shard_map/transpose | solution.py:296
  1.7 1.0 %copy.8 = bf16[3,3,3,64,64]{4,3,2,1,0:T(8,128)(2,1)} copy(bf16[3,3,3,64,64]{3,4,2,1,0:T(8,128)(2,1)S(1)} %reverse_bitcast_fusion.1) | data formatting | bytes 442368 | tf_op jit(solution)/shard_map/transpose | solution.py:296
  2.7 0.0 copy-done.1
  2.8 0.2 copy.9
  3.0 0.2 copy.11
  3.2 0.2 copy.10
  3.5 1.1 %pad_maximum_fusion.wg = bf16[1152,192]{1,0:T(8,128)(2,1)} fusion(bf16[1152,64]{1,0:T(8,128)(2,1)S(1)} %bitcast.26, bf16[1152,64]{1,0:T(8,128)(2,1)S(1)} %bitcast.27, bf16[1152,64]{1,0:T(8,128)(2,1)S(1)} %bitcast.25), kind=kLoop, calls=%fused_computation | loop fusion | flops 1327104 | bytes 884736 | tf_op jit(solution)/shard_map/concatenate | solution.py:298
  4.6 77.8 %shard_map.75 = (f32[4096,128]{1,0:T(8,128)}, f32[4096,64]{1,0:T(8,128)}, f32[27,4,64]{2,1,0:T(4,128)}, f32[27,8,64]{2,1,0:T(8,128)}) custom-call(bf16[4096,64]{1,0:T(8,128)(2,1)} %bitcast.28, bf16[4096,128]{1,0:T(8,128)(2,1)} %bitcast.29, bf16[9,192,64]{2,1,0:T(8,128)(2,1)} %bitcast.22, bf16[9,192,128]{2,1,0:T(8,128)(2,1)} %bitcast.23, ...), custom_call_target="tpu_custom_call" | custom-call | tf_op jit(solution)/shard_map/pallas_call | solution.py:304
  82.3 0.0 copy-start
  82.4 3.2 %copy.16 = f32[2,64,32,128]{3,2,1,0:T(8,128)} copy(f32[2,64,32,128]{3,2,1,0:T(8,128)} %bitcast.21) | data formatting | bytes 4194304
  85.6 0.0 copy-done
  85.6 0.0 copy-start.3
  85.6 0.0 copy-start.2
  85.6 1.3 %copy.17 = f32[2,64,32,64]{3,2,1,0:T(8,128)} copy(f32[2,64,32,64]{3,2,1,0:T(8,128)S(1)} %bitcast.20) | data formatting | bytes 2097152
  86.9 0.0 copy-done.3
  86.9 0.6 copy.18
  87.5 0.0 copy-done.2
  87.5 0.6 copy.19
  (2 shorter events, 0.1 us)
Async XLA Ops:
  0.6 2.1 %copy-start.1 = (bf16[3,3,3,64,128]{4,3,2,1,0:T(8,128)(2,1)S(1)}, bf16[3,3,3,64,128]{4,3,2,1,0:T(8,128)(2,1)}, u32[]{:S(2)}) copy-start(bf16[3,3,3,64,128]{4,3,2,1,0:T(8,128)(2,1)} %param.6) | copy-start | bytes 1327108
  82.3 3.2 %copy-start = (f32[4096,64]{1,0:T(8,128)S(1)}, f32[4096,64]{1,0:T(8,128)}, u32[]{:S(2)}) copy-start(f32[4096,64]{1,0:T(8,128)} %get-tuple-element.9) | copy-start | bytes 3145732
  85.6 1.3 %copy-start.3 = (f32[27,4,64]{2,1,0:T(4,128)S(1)}, f32[27,4,64]{2,1,0:T(4,128)}, u32[]{:S(2)}) copy-start(f32[27,4,64]{2,1,0:T(4,128)} %get-tuple-element.10) | copy-start | bytes 82948
  85.6 1.9 %copy-start.2 = (f32[27,8,64]{2,1,0:T(8,128)S(1)}, f32[27,8,64]{2,1,0:T(8,128)}, u32[]{:S(2)}) copy-start(f32[27,8,64]{2,1,0:T(8,128)} %get-tuple-element.11) | copy-start | bytes 165892
where the time goes:
time: 88.3 us; the launch traced here: 88.2 us
  Pallas kernels  77.8 us (88%)
  local copies, waits for them, and re-layouts  8.65 us (10%)
  other arithmetic  1.1 us (1%)
    pallas_call x1, Pallas kernels, shards(): pl.pallas_call(functools.partial(kernel, n, planes, height, width, ci, cm...  77.8 us
    unnamed x12, local copies, waits for them, and re-layouts  5.83 us
    transpose x2, local copies, waits for them, and re-layouts, shards(): jnp.transpose(weight_one[::-1, ::-1, ::-1], (0, 1, 2, 4, 3))  2.06 us

commit v1 on v0

--- a/solution.py
+++ b/solution.py
@@ -16,10 +16,11 @@
 
 def kernel(
     n, planes, height, width, ci, cm, co, scale,
-    vol, cot, w1, w2, w1f, wg,
+    vol, cot, w1, w2,
     out, gvol, g1, g2,
-    pv, pa, pg, ct, vraw, araw, graw, vh, ah, gh, dsl, acc1, acc2, tx, rx,
-    loc_sem, hs_sem, hr_sem, ts_sem, tr_sem,
+    pv, pa, pg, ct, vraw, araw, graw, vs, sa, gs, vh, ah, gh, dsl, acc1, acc2,
+    w1f, wg, own, tx, rx, ty, ry,
+    loc_sem, hs_sem, hr_sem, ps_sem, pr_sem, ts_sem, tr_sem,
 ):
     me = lax.axis_index("space")
     plane = height * width
@@ -45,6 +46,14 @@
     for copy in local:
         copy.start()
 
+    for t in range(9):
+        w = w2[8 - t]
+        order = [w[2 * cm :], w[:cm], w[cm : 2 * cm]]
+        wg[pl.ds(t * co, co), :] = jnp.concatenate(order, axis=0).T
+        w = w1[8 - t]
+        for c in range(3):
+            w1f[t, pl.ds(c * cm, cm), :] = w[(2 - c) * ci : (3 - c) * ci].T
+
     for ref in (pv, pa, pg, ct):
         zero = jnp.zeros((width, ref.shape[2]), BF16)
         for p in range(planes + 2):
@@ -116,25 +125,36 @@
 
     end = (planes - 1) * plane
     volume_halo = halo(
-        0, vol.at[pl.ds(0, plane)], vol.at[pl.ds(end, plane)], vh.at[0], vh.at[1]
+        0, vs.at[0], vs.at[1], vh.at[0], vh.at[1]
     )
     cot_halo = halo(
         1, cot.at[pl.ds(0, plane)], cot.at[pl.ds(end, plane)],
         ct.at[0, pl.ds(width, plane)], ct.at[planes + 1, pl.ds(width, plane)],
     )
     act_halo = halo(
-        2, araw.at[pl.ds(0, plane)], araw.at[pl.ds(end, plane)], ah.at[0], ah.at[1]
+        2, sa.at[0], sa.at[1], ah.at[0], ah.at[1]
     )
     grad_halo = halo(
-        3, graw.at[pl.ds(0, plane)], graw.at[pl.ds(end, plane)], gh.at[0], gh.at[1]
-    )
+        3, gs.at[0], gs.at[1], gh.at[0], gh.at[1]
+    )
+
+    local[0].wait()
+
+    def pack(raw, ref):
+        for side, start in enumerate((0, end)):
+            for k in range(2):
+                low = raw[pl.ds(start + k * chunk, chunk), :].astype(F32)
+                high = raw[pl.ds(start + (2 + k) * chunk, chunk), :].astype(F32)
+                ref[side, pl.ds(k * chunk, chunk), :] = jnp.concatenate(
+                    [low, high], axis=1
+                ).astype(BF16)
+
+    pack(vraw, vs)
 
     pl.semaphore_wait(barrier, n - 1)
     volume_halo[0]()
     cot_halo[0]()
 
-    local[0].wait()
-
     def own_volume(p, row):
         x = vraw[pl.ds(pl.multiple_of(p * plane + row, chunk), chunk), :].astype(F32)
         spread(x, pv, p + 1, row + width)
@@ -142,15 +162,18 @@
     each(planes, own_volume)
 
     def halo_planes(slots, ref):
-        def body(p, row):
+        def body(k, carry):
+            p, row = k // 2, pl.multiple_of(lax.rem(k, 2) * chunk, chunk)
             x = slots[p, pl.ds(row, chunk), :].astype(F32)
-            spread(x, ref, p * (planes + 1), row + width)
-
-        each(2, body)
-
-    def conv(ref, kernels, p, row):
-        total = None
-        for a in range(3):
+            half = x.shape[1] // 2
+            spread(x[:, :half], ref, p * (planes + 1), row + width)
+            spread(x[:, half:], ref, p * (planes + 1), row + width + 2 * chunk)
+            return carry
+
+        lax.fori_loop(0, 4, body, 0)
+
+    def conv(ref, kernels, p, row, taps=(0, 1, 2), total=None):
+        for a in taps:
             for b in range(3):
                 term = jnp.dot(
                     ref[p + a, pl.ds(pl.multiple_of(row + b * width, width), chunk), :],
@@ -160,19 +183,40 @@
                 total = term if total is None else total + term
         return total
 
+    def parted(p):
+        inner = [a for a in range(3) if 1 <= p + a <= planes]
+        return inner, [a for a in range(3) if a not in inner]
+
+    def chunks(body):
+        def step(k, carry):
+            body(pl.multiple_of(k * chunk, chunk))
+            return carry
+
+        lax.fori_loop(0, 4, step, 0)
+
+    for p in range(planes):
+
+        def inner_conv(row, p=p):
+            at = pl.ds(pl.multiple_of(p * plane + row, chunk), chunk)
+            dsl[at, :] = conv(pv, w1, p, row, parted(p)[0])
+
+        chunks(inner_conv)
+
     volume_halo[1]()
     halo_planes(vh, pv)
 
     def first_conv(p, row):
-        hidden = conv(pv, w1, p, row)
+        at = pl.ds(pl.multiple_of(p * plane + row, chunk), chunk)
+        hidden = conv(pv, w1, p, row, parted(p)[1], dsl[at, :])
         s = jax.nn.sigmoid(hidden)
-        at = pl.ds(pl.multiple_of(p * plane + row, chunk), chunk)
         dsl[at, :] = s * (1.0 + hidden * (1.0 - s))
         rounded = (hidden * s).astype(BF16)
         araw[at, :] = rounded
         spread(rounded.astype(F32), pa, p + 1, row + width)
 
-    each(planes, first_conv)
+    for p in range(planes):
+        chunks(functools.partial(first_conv, p))
+    pack(araw, sa)
     act_halo[0]()
 
     for copy in local[1:]:
@@ -200,6 +244,7 @@
         spread(rounded.astype(F32), pg, p + 1, row + width)
 
     each(planes, back_conv)
+    pack(graw, gs)
     grad_halo[0]()
 
     act_halo[1]()
@@ -220,38 +265,58 @@
 
     each(planes, kernel_terms)
 
-    blank = jnp.zeros((tx.shape[2] - r1 - r2, 3 * ci), F32)
-    for t in range(9):
-        for s in range(n):
-            tile = jnp.concatenate(
-                [
-                    acc2[t, pl.ds(s * r2, r2), :],
-                    acc1[t, pl.ds(s * r1, r1), :],
-                    blank,
-                ],
-                axis=0,
-            ).astype(BF16)
-            tx[s, t] = tile[:, : 2 * ci]
-            tx[s, 9 + t // 2, :, pl.ds((t % 2) * ci, ci)] = tile[:, 2 * ci :]
-    for s in range(n):
-        tx[s, 13, :, pl.ds(ci, ci)] = jnp.zeros((tx.shape[2], ci), BF16)
-
-    sends = []
-    for j in range(1, n):
-        owner = lax.rem(me + j, n)
-        sends.append(
-            pltpu.make_async_remote_copy(
-                tx.at[owner], rx.at[j], ts_sem.at[j], tr_sem.at[j],
-                device_id={"space": owner}, device_id_type=MESH,
-            )
-        )
-        sends[-1].start()
+    parity = lax.rem(me, 2)
+    mine = me // 2
+    used = 14 * (r1 + r2)
+    for d in range(n):
+        pieces = []
+        for acc, r in ((acc2, r2), (acc1, r1)):
+            taps = [acc[t, pl.ds(d * r, r), :] for t in range(9)]
+            pieces += [x[:, : 2 * ci] for x in taps]
+            last_taps = [x[:, 2 * ci :] for x in taps] + [jnp.zeros((r, ci), F32)]
+            pieces += [
+                jnp.concatenate(last_taps[2 * k : 2 * k + 2], axis=1) for k in range(5)
+            ]
+        if tx.shape[2] > used:
+            pieces.append(jnp.zeros((tx.shape[2] - used, 2 * ci), F32))
+        whole = jnp.concatenate(pieces, axis=0)
+        own[d % 2, d // 2] = whole
+        tx[d % 2, d // 2] = whole.astype(BF16)
+
+    pair = pltpu.make_async_remote_copy(
+        tx.at[1 - parity], rx, ps_sem.at[0], pr_sem.at[0],
+        device_id={"space": me + 1 - 2 * parity}, device_id_type=MESH,
+    )
+    pair.start()
 
     def second_conv(p, row):
         at = pl.ds(pl.multiple_of(p * plane + row, chunk), chunk)
         out[at, :] = conv(pa, w2, p, row)
 
-    each(planes, second_conv)
+    each(1, second_conv)
+
+    pair.wait_recv()
+
+    def pair_sum(m, carry):
+        ty[m] = (own[parity, m] + rx[m].astype(F32)).astype(BF16)
+        return carry
+
+    lax.fori_loop(0, n // 2, pair_sum, 0)
+    sends = []
+    for j in range(1, n // 2):
+        slot = lax.rem(mine + j, n // 2)
+        sends.append(
+            pltpu.make_async_remote_copy(
+                ty.at[slot], ry.at[j], ts_sem.at[j], tr_sem.at[j],
+                device_id={"space": 2 * slot + parity}, device_id_type=MESH,
+            )
+        )
+        sends[-1].start()
+
+    def rest_second(p, row):
+        second_conv(p + 1, row)
+
+    each(planes - 1, rest_second)
 
     grad_halo[1]()
     halo_planes(gh, pg)
@@ -264,18 +329,19 @@
 
     for send in sends:
         send.wait_recv()
+    total = own[parity, mine] + rx[mine].astype(F32)
+    for j in range(1, n // 2):
+        total = total + ry[j].astype(F32)
+    total = total * scale
     for t in range(14):
-        total = tx[me, t].astype(F32)
-        for j in range(1, n):
-            total = total + rx[j, t].astype(F32)
-        total = total * scale
-        taps = (3 * t, 3 * t + 1) if t < 9 else (3 * (2 * (t - 9)) + 2, 3 * (2 * (t - 9) + 1) + 2)
+        taps = (3 * t, 3 * t + 1) if t < 9 else (6 * (t - 9) + 2, 6 * (t - 9) + 5)
         for half, tap in enumerate(taps):
             if tap < 27:
-                part = total[:, half * ci : (half + 1) * ci]
-                g2[tap] = part[:r2]
-                g1[tap] = part[r2 : r2 + r1]
-
+                lanes = slice(half * ci, (half + 1) * ci)
+                g2[tap] = total[t * r2 : (t + 1) * r2, lanes]
+                g1[tap] = total[14 * r2 + t * r1 : 14 * r2 + (t + 1) * r1, lanes]
+
+    pair.wait_send()
     for send in sends:
         send.wait_send()
     for exchange in (volume_halo, cot_halo, act_halo, grad_halo):
@@ -293,14 +359,10 @@
 
     w1 = weight_one.reshape(9, 3 * ci, cm)
     w2 = weight_two.reshape(9, 3 * cm, co)
-    w1f = jnp.transpose(weight_one[::-1, ::-1, ::-1], (0, 1, 2, 4, 3)).reshape(9, 3 * cm, ci)
-    wg = jnp.transpose(weight_two[::-1, ::-1, ::-1], (0, 1, 4, 2, 3))
-    wg = jnp.concatenate([wg[:, :, :, 0], wg[:, :, :, 2], wg[:, :, :, 1]], axis=3)
-    wg = wg.reshape(9 * co, 3 * cm)
 
     vmem = pl.BlockSpec(memory_space=pltpu.VMEM)
     hbm = pl.BlockSpec(memory_space=pl.ANY)
-    rows = -(-(cm // n + co // n) // 16) * 16
+    rows = -(-14 * (cm // n + co // n) // 16) * 16
     out, gvol, g1, g2 = pl.pallas_call(
         functools.partial(kernel, n, planes, height, width, ci, cm, co, scale),
         out_shape=(
@@ -309,7 +371,7 @@
             jax.ShapeDtypeStruct((27, cm // n, ci), F32),
             jax.ShapeDtypeStruct((27, co // n, cm), F32),
         ),
-        in_specs=[hbm, hbm, vmem, vmem, vmem, vmem],
+        in_specs=[hbm, hbm, vmem, vmem],
         out_specs=(vmem, vmem, vmem, vmem),
         scratch_shapes=[
             pltpu.VMEM((planes + 2, pad, 3 * ci), BF16),
@@ -319,25 +381,35 @@
             pltpu.VMEM((cells, ci), BF16),
             pltpu.VMEM((cells, cm), BF16),
             pltpu.VMEM((cells, cm), BF16),
-            pltpu.VMEM((2, plane, ci), BF16),
-            pltpu.VMEM((2, plane, cm), BF16),
-            pltpu.VMEM((2, plane, cm), BF16),
+            pltpu.VMEM((2, plane // 2, 2 * ci), BF16),
+            pltpu.VMEM((2, plane // 2, 2 * cm), BF16),
+            pltpu.VMEM((2, plane // 2, 2 * cm), BF16),
+            pltpu.VMEM((2, plane // 2, 2 * ci), BF16),
+            pltpu.VMEM((2, plane // 2, 2 * cm), BF16),
+            pltpu.VMEM((2, plane // 2, 2 * cm), BF16),
             pltpu.VMEM((cells, cm), F32),
             pltpu.VMEM((9, cm, 3 * ci), F32),
             pltpu.VMEM((9, co, 3 * cm), F32),
-            pltpu.VMEM((n, 14, rows, 2 * ci), BF16),
-            pltpu.VMEM((n, 14, rows, 2 * ci), BF16),
+            pltpu.VMEM((9, 3 * cm, ci), BF16),
+            pltpu.VMEM((9 * co, 3 * cm), BF16),
+            pltpu.VMEM((2, n // 2, rows, 2 * ci), F32),
+            pltpu.VMEM((2, n // 2, rows, 2 * ci), BF16),
+            pltpu.VMEM((n // 2, rows, 2 * ci), BF16),
+            pltpu.VMEM((n // 2, rows, 2 * ci), BF16),
+            pltpu.VMEM((n // 2, rows, 2 * ci), BF16),
             pltpu.SemaphoreType.DMA((1 + planes,)),
             pltpu.SemaphoreType.DMA((4, 2)),
             pltpu.SemaphoreType.DMA((4, 2)),
-            pltpu.SemaphoreType.DMA((n,)),
-            pltpu.SemaphoreType.DMA((n,)),
+            pltpu.SemaphoreType.DMA((1,)),
+            pltpu.SemaphoreType.DMA((1,)),
+            pltpu.SemaphoreType.DMA((n // 2,)),
+            pltpu.SemaphoreType.DMA((n // 2,)),
         ],
         compiler_params=pltpu.CompilerParams(
-            collective_id=0, has_side_effects=True, vmem_limit_bytes=60 << 20
+            collective_id=0, has_side_effects=True, vmem_limit_bytes=38 << 20
         ),
     )(
-        volume.reshape(cells, ci), cotangent.reshape(cells, co), w1, w2, w1f, wg
+        volume.reshape(cells, ci), cotangent.reshape(cells, co), w1, w2
     )
     return (
         out.reshape(planes, height, width, co),

time: 88.3 us -> 65.3 us (0.74)
  the two profiles are of different devices: /device:TPU:1 before, /device:TPU:4 now
where the time goes in v1:
time: 65.3 us; the launch traced here: 65 us
  Pallas kernels  56 us (86%)
  local copies, waits for them, and re-layouts  8.37 us (13%)
    pallas_call x1, Pallas kernels, shards(): pl.pallas_call(functools.partial(kernel, n, planes, height, width, ci, cm...  56 us
    unnamed x12, local copies, waits for them, and re-layouts  8.37 us

profile of v1, /device:TPU:4, one launch (start us, length us, event | category | flops | bytes accessed | tf_op | source)
XLA Modules:
  0.0 65.0 jit_solution(11337584668537678777)
XLA Ops:
  0.6 0.0 copy-start
  0.6 1.2 %copy-done = bf16[2,64,32,64]{3,2,1,0:T(8,128)(2,1)S(1)} copy-done((bf16[2,64,32,64]{3,2,1,0:T(8,128)(2,1)S(1)}, bf16[2,64,32,64]{3,2,1,0:T(8,128)(2,1)}, u32[]{:S(2)}) %copy-start) | copy-done | bytes 524312
  1.9 0.0 copy-start.1
  1.9 1.2 %copy-done.1 = bf16[2,64,32,128]{3,2,1,0:T(8,128)(2,1)S(1)} copy-done((bf16[2,64,32,128]{3,2,1,0:T(8,128)(2,1)S(1)}, bf16[2,64,32,128]{3,2,1,0:T(8,128)(2,1)}, u32[]{:S(2)}) %copy-start.1) | copy-done | bytes 1048600
  3.1 0.0 copy-start.2
  3.1 1.0 %copy-done.2 = bf16[3,3,3,64,64]{4,3,2,1,0:T(8,128)(2,1)S(1)} copy-done((bf16[3,3,3,64,64]{4,3,2,1,0:T(8,128)(2,1)S(1)}, bf16[3,3,3,64,64]{4,3,2,1,0:T(8,128)(2,1)}, u32[]{:S(2)}) %copy-start.2) | copy-done | bytes 221208
  4.1 0.0 copy-start.3
  4.1 1.0 %copy-done.3 = bf16[3,3,3,64,128]{4,3,2,1,0:T(8,128)(2,1)S(1)} copy-done((bf16[3,3,3,64,128]{4,3,2,1,0:T(8,128)(2,1)S(1)}, bf16[3,3,3,64,128]{4,3,2,1,0:T(8,128)(2,1)}, u32[]{:S(2)}) %copy-start.3) | copy-done | bytes 442392
  5.1 56.0 %shard_map.75 = (f32[4096,128]{1,0:T(8,128)S(1)}, f32[4096,64]{1,0:T(8,128)S(1)}, f32[27,4,64]{2,1,0:T(4,128)S(1)}, f32[27,8,64]{2,1,0:T(8,128)S(1)}) custom-call(bf16[4096,64]{1,0:T(8,128)(2,1)S(1)} %bitcast.14, bf16[4096,128]{1,0:T(8,128)(2,1)S(1)} %bitcast.15, bf16[9,192,64]{2,1,0:T(8,128)(2,1)S(1)} %bitcast.16, bf16[9,192,128]{2,1,0:T(8,128)(2,1)S(1)} %bitcast.17), custom_call_target="tpu_custom_call" | custom-call | tf_op jit(solution)/shard_map/pallas_call | solution.py:366
  61.1 1.3 %copy.12 = f32[2,64,32,128]{3,2,1,0:T(8,128)} copy(f32[2,64,32,128]{3,2,1,0:T(8,128)S(1)} %bitcast.13) | data formatting | bytes 4194304
  62.5 1.3 %copy.13 = f32[2,64,32,64]{3,2,1,0:T(8,128)} copy(f32[2,64,32,64]{3,2,1,0:T(8,128)S(1)} %bitcast.12) | data formatting | bytes 2097152
  63.8 0.6 copy.14
  64.4 0.6 copy.15
Async XLA Ops:
  0.6 1.2 %copy-start = (bf16[2,64,32,64]{3,2,1,0:T(8,128)(2,1)S(1)}, bf16[2,64,32,64]{3,2,1,0:T(8,128)(2,1)}, u32[]{:S(2)}) copy-start(bf16[2,64,32,64]{3,2,1,0:T(8,128)(2,1)} %param.4) | copy-start | bytes 1572868
  1.9 1.2 %copy-start.1 = (bf16[2,64,32,128]{3,2,1,0:T(8,128)(2,1)S(1)}, bf16[2,64,32,128]{3,2,1,0:T(8,128)(2,1)}, u32[]{:S(2)}) copy-start(bf16[2,64,32,128]{3,2,1,0:T(8,128)(2,1)} %param.7) | copy-start | bytes 3145732
  3.1 1.0 %copy-start.2 = (bf16[3,3,3,64,64]{4,3,2,1,0:T(8,128)(2,1)S(1)}, bf16[3,3,3,64,64]{4,3,2,1,0:T(8,128)(2,1)}, u32[]{:S(2)}) copy-start(bf16[3,3,3,64,64]{4,3,2,1,0:T(8,128)(2,1)} %param.5) | copy-start | bytes 663556
  4.1 1.0 %copy-start.3 = (bf16[3,3,3,64,128]{4,3,2,1,0:T(8,128)(2,1)S(1)}, bf16[3,3,3,64,128]{4,3,2,1,0:T(8,128)(2,1)}, u32[]{:S(2)}) copy-start(bf16[3,3,3,64,128]{4,3,2,1,0:T(8,128)(2,1)} %param.6) | copy-start | bytes 1327108

commit v2 on v1

--- a/solution.py
+++ b/solution.py
@@ -16,11 +16,11 @@
 
 def kernel(
     n, planes, height, width, ci, cm, co, scale,
-    vol, cot, w1, w2,
-    out, gvol, g1, g2,
-    pv, pa, pg, ct, vraw, araw, graw, vs, sa, gs, vh, ah, gh, dsl, acc1, acc2,
-    w1f, wg, own, tx, rx, ty, ry,
-    loc_sem, hs_sem, hr_sem, ps_sem, pr_sem, ts_sem, tr_sem,
+    vol, cot, w1_in, w2_in,
+    out_hbm, gvol_hbm, g1, g2,
+    out, gvol, pv, pa, pg, ct, vraw, araw, graw, vs, sa, gs, vh, ah, gh, dsl, acc1, acc2,
+    w1, w2, w1f, wg, own, tx, rx, ty, ry,
+    loc_sem, st_sem, hs_sem, hr_sem, ps_sem, pr_sem, ts_sem, tr_sem,
 ):
     me = lax.axis_index("space")
     plane = height * width
@@ -43,8 +43,15 @@
                 loc_sem.at[1 + p],
             )
         )
-    for copy in local:
+    weights = [
+        pltpu.make_async_copy(w2_in, w2, loc_sem.at[1 + planes]),
+        pltpu.make_async_copy(w1_in, w1, loc_sem.at[2 + planes]),
+    ]
+    for copy in local[:1] + weights + local[1:]:
         copy.start()
+
+    for copy in weights:
+        copy.wait()
 
     for t in range(9):
         w = w2[8 - t]
@@ -294,6 +301,14 @@
         out[at, :] = conv(pa, w2, p, row)
 
     each(1, second_conv)
+    stores = [
+        pltpu.make_async_copy(
+            out.at[pl.ds(lo, size)], out_hbm.at[pl.ds(lo, size)], st_sem.at[k]
+        )
+        for k, (lo, size) in enumerate(((0, plane), (plane, (planes - 1) * plane)))
+    ]
+    stores.append(pltpu.make_async_copy(gvol, gvol_hbm, st_sem.at[2]))
+    stores[0].start()
 
     pair.wait_recv()
 
@@ -317,6 +332,7 @@
         second_conv(p + 1, row)
 
     each(planes - 1, rest_second)
+    stores[1].start()
 
     grad_halo[1]()
     halo_planes(gh, pg)
@@ -326,6 +342,7 @@
         gvol[at, :] = conv(pg, w1f, p, row)
 
     each(planes, last_conv)
+    stores[2].start()
 
     for send in sends:
         send.wait_recv()
@@ -341,6 +358,8 @@
                 g2[tap] = total[t * r2 : (t + 1) * r2, lanes]
                 g1[tap] = total[14 * r2 + t * r1 : 14 * r2 + (t + 1) * r1, lanes]
 
+    for store in stores:
+        store.wait()
     pair.wait_send()
     for send in sends:
         send.wait_send()
@@ -361,7 +380,7 @@
     w2 = weight_two.reshape(9, 3 * cm, co)
 
     vmem = pl.BlockSpec(memory_space=pltpu.VMEM)
-    hbm = pl.BlockSpec(memory_space=pl.ANY)
+    hbm = pl.BlockSpec(memory_space=pltpu.HBM)
     rows = -(-14 * (cm // n + co // n) // 16) * 16
     out, gvol, g1, g2 = pl.pallas_call(
         functools.partial(kernel, n, planes, height, width, ci, cm, co, scale),
@@ -371,9 +390,11 @@
             jax.ShapeDtypeStruct((27, cm // n, ci), F32),
             jax.ShapeDtypeStruct((27, co // n, cm), F32),
         ),
-        in_specs=[hbm, hbm, vmem, vmem],
-        out_specs=(vmem, vmem, vmem, vmem),
+        in_specs=[hbm, hbm, hbm, hbm],
+        out_specs=(hbm, hbm, vmem, vmem),
         scratch_shapes=[
+            pltpu.VMEM((cells, co), F32),
+            pltpu.VMEM((cells, ci), F32),
             pltpu.VMEM((planes + 2, pad, 3 * ci), BF16),
             pltpu.VMEM((planes + 2, pad, 3 * cm), BF16),
             pltpu.VMEM((planes + 2, pad, 3 * cm), BF16),
@@ -390,6 +411,8 @@
             pltpu.VMEM((cells, cm), F32),
             pltpu.VMEM((9, cm, 3 * ci), F32),
             pltpu.VMEM((9, co, 3 * cm), F32),
+            pltpu.VMEM((9, 3 * ci, cm), BF16),
+            pltpu.VMEM((9, 3 * cm, co), BF16),
             pltpu.VMEM((9, 3 * cm, ci), BF16),
             pltpu.VMEM((9 * co, 3 * cm), BF16),
             pltpu.VMEM((2, n // 2, rows, 2 * ci), F32),
@@ -397,7 +420,8 @@
             pltpu.VMEM((n // 2, rows, 2 * ci), BF16),
             pltpu.VMEM((n // 2, rows, 2 * ci), BF16),
             pltpu.VMEM((n // 2, rows, 2 * ci), BF16),
-            pltpu.SemaphoreType.DMA((1 + planes,)),
+            pltpu.SemaphoreType.DMA((3 + planes,)),
+            pltpu.SemaphoreType.DMA((3,)),
             pltpu.SemaphoreType.DMA((4, 2)),
             pltpu.SemaphoreType.DMA((4, 2)),
             pltpu.SemaphoreType.DMA((1,)),
@@ -406,7 +430,7 @@
             pltpu.SemaphoreType.DMA((n // 2,)),
         ],
         compiler_params=pltpu.CompilerParams(
-            collective_id=0, has_side_effects=True, vmem_limit_bytes=38 << 20
+            collective_id=0, has_side_effects=True, vmem_limit_bytes=60 << 20
         ),
     )(
         volume.reshape(cells, ci), cotangent.reshape(cells, co), w1, w2

time: 65.3 us -> 64.6 us (0.989)
  local copies, waits for them, and re-layouts: 8.37 us -> 5.83 us
  Pallas kernels: 56 us -> 57.9 us
    unnamed x12 -> x10, local copies, waits for them, and re-layouts: 8.37 us -> 5.83 us
    pallas_call x1, Pallas kernels: 56 us -> 57.9 us  [shards(): pl.pallas_call(functools.partial(kernel, n, planes, height, width, ci, cm...]
where the time goes in v2:
time: 64.6 us; the launch traced here: 64.4 us
  Pallas kernels  57.9 us (90%)
  local copies, waits for them, and re-layouts  5.83 us (9%)
  between operations  0.65 us (1%)
    pallas_call x1, Pallas kernels, shards(): pl.pallas_call(functools.partial(kernel, n, planes, height, width, ci, cm...  57.9 us
    unnamed x10, local copies, waits for them, and re-layouts  5.83 us

profile of v2, /device:TPU:4, one launch (start us, length us, event | category | flops | bytes accessed | tf_op | source)
XLA Modules:
  0.0 64.4 jit_solution(12688877086312353577)
XLA Ops:
  0.6 57.9 %shard_map.75 = (f32[4096,128]{1,0:T(8,128)}, f32[4096,64]{1,0:T(8,128)}, f32[27,4,64]{2,1,0:T(4,128)}, f32[27,8,64]{2,1,0:T(8,128)}) custom-call(bf16[4096,64]{1,0:T(8,128)(2,1)} %bitcast.14, bf16[4096,128]{1,0:T(8,128)(2,1)} %bitcast.15, bf16[9,192,64]{2,1,0:T(8,128)(2,1)} %bitcast.16, bf16[9,192,128]{2,1,0:T(8,128)(2,1)} %bitcast.17), custom_call_target="tpu_custom_call" | custom-call | tf_op jit(solution)/shard_map/pallas_call | solution.py:385
  58.6 0.0 copy-start
  58.6 3.2 %copy.12 = f32[2,64,32,128]{3,2,1,0:T(8,128)} copy(f32[2,64,32,128]{3,2,1,0:T(8,128)} %bitcast.13) | data formatting | bytes 4194304
  61.8 0.0 copy-done
  61.8 0.0 copy-start.2
  61.8 0.0 copy-start.1
  61.8 1.3 %copy.13 = f32[2,64,32,64]{3,2,1,0:T(8,128)} copy(f32[2,64,32,64]{3,2,1,0:T(8,128)S(1)} %bitcast.12) | data formatting | bytes 2097152
  63.1 0.0 copy-done.2
  63.1 0.6 copy.14
  63.8 0.0 copy-done.1
  63.8 0.6 %copy.15 = f32[3,3,3,64,8]{3,4,2,1,0:T(8,128)} copy(f32[3,3,3,64,8]{3,4,2,1,0:T(8,128)S(1)} %bitcast.18) | data formatting | bytes 110592
Async XLA Ops:
  58.6 3.2 %copy-start = (f32[4096,64]{1,0:T(8,128)S(1)}, f32[4096,64]{1,0:T(8,128)}, u32[]{:S(2)}) copy-start(f32[4096,64]{1,0:T(8,128)} %get-tuple-element.9) | copy-start | bytes 3145732
  61.8 1.3 %copy-start.2 = (f32[27,4,64]{2,1,0:T(4,128)S(1)}, f32[27,4,64]{2,1,0:T(4,128)}, u32[]{:S(2)}) copy-start(f32[27,4,64]{2,1,0:T(4,128)} %get-tuple-element.10) | copy-start | bytes 82948
  61.8 1.9 %copy-start.1 = (f32[27,8,64]{2,1,0:T(8,128)S(1)}, f32[27,8,64]{2,1,0:T(8,128)}, u32[]{:S(2)}) copy-start(f32[27,8,64]{2,1,0:T(8,128)} %get-tuple-element.11) | copy-start | bytes 165892
